TPU v7x, 256 devices: a whole 4x4x8 slice. The times are simulated.
256 devices in a mesh: dp: 16 (over x_lo, y, core), ctx: 16 (over z, x_hi).
Axes of the slice: x: 4 (x_hi: 2, x_lo: 2; x = x_hi * 2 + x_lo), y: 4, z: 8, core: 2. Of those that a mesh axis runs over, the one named last changes fastest.
Arguments:
- input_gate: bfloat16 [512, 131072], P('dp', 'ctx'), may hold values from -6 to 6
- output_gate: bfloat16 [512, 131072], P('dp', 'ctx'), may hold values from -6 to 6
- values: bfloat16 [512, 131072], P('dp', 'ctx'), may hold values from -6 to 6
- cotangent: bfloat16 [512, 131072], P('dp', 'ctx'), may hold values from -6 to 6
- filter_raw: bfloat16 [16, 131072], P(None, 'ctx'), may hold values from -6 to 6
- filter_decay: float32 [16], replicated, may hold values from 0.25 to 2
- skip_gain: float32 [512], P('dp'), may hold values from -4 to 4
Outputs:
- outputs: bfloat16 [512, 131072], P('dp', 'ctx')
- grad_input_gate: bfloat16 [512, 131072], P('dp', 'ctx')
- grad_output_gate: bfloat16 [512, 131072], P('dp', 'ctx')
- grad_values: bfloat16 [512, 131072], P('dp', 'ctx')
- grad_filter: float32 [16, 131072], P(None, 'ctx')
All inputs are finite; a program needn't handle non-finite values.
Results may differ from a plain program's by a relative error of at most 0.018.
Values may be sent and summed in bfloat16 or wider, within the bound.
A program may use at most 64 MiB of HBM per device.

v0:
```python
import math

import jax
import jax.numpy as jnp
from jax import lax
from jax.sharding import PartitionSpec as P

N1 = 512
N2 = 512
FFT_LEN = 262144


two_pi = 2.0 * math.pi


def over_pieces(x, axis):
    return lax.all_gather(x, axis).astype(jnp.float32).sum(0)


def first_tables(row_total):
    first_index = jnp.arange(N1, dtype=jnp.int32)
    source_rows = jnp.arange(row_total, dtype=jnp.int32)
    angles = (first_index[:, None] * source_rows[None, :] % N1).astype(jnp.float32) * (two_pi / N1)
    cosine = jnp.cos(angles).astype(jnp.bfloat16)
    minus_sine = (-jnp.sin(angles)).astype(jnp.bfloat16)
    forward_table = jnp.concatenate([cosine, minus_sine], axis=0)
    inverse_table = jnp.stack([cosine.T, minus_sine.T], axis=2)
    return (forward_table, inverse_table)


def second_tables():
    second_index = jnp.arange(N2, dtype=jnp.int32)
    angles = (second_index[:, None] * second_index[None, :] % N2).astype(jnp.float32) * (
        two_pi / N2
    )
    cosine = jnp.cos(angles).astype(jnp.bfloat16)
    minus_sine = (-jnp.sin(angles)).astype(jnp.bfloat16)
    forward_table = jnp.stack(
        [
            jnp.concatenate([cosine, minus_sine], axis=1),
            jnp.concatenate([-minus_sine, cosine], axis=1),
        ],
        axis=0,
    )
    inverse_table = jnp.concatenate(
        [
            jnp.concatenate([cosine, -minus_sine], axis=1),
            jnp.concatenate([minus_sine, cosine], axis=1),
        ],
        axis=0,
    )
    return (forward_table, inverse_table)


def twiddle_table(spectrum_rows, columns):
    angles = (spectrum_rows[:, None] * columns[None, :] % FFT_LEN).astype(jnp.float32) * (
        two_pi / FFT_LEN
    )
    return (jnp.cos(angles), -jnp.sin(angles))


def halves(array):
    return (array[..., :N2], array[..., N2:])


def joined(real_part, imaginary_part):
    return jnp.concatenate([real_part, imaginary_part], axis=-1).astype(jnp.bfloat16)


def spectral_products(mix_spec, weight_spec, filter_spec, which):
    lead = mix_spec.shape[:-2]
    filters = filter_spec.shape[-2]
    filter_real, filter_imaginary = halves(filter_spec.astype(jnp.float32))
    filter_real = jnp.expand_dims(filter_real, -3)
    filter_imaginary = jnp.expand_dims(filter_imaginary, -3)
    outcome = []
    mix_real, mix_imaginary = halves(mix_spec.reshape(lead + (-1, filters, 2 * N2)))
    weight_real, weight_imaginary = halves(weight_spec.reshape(lead + (-1, filters, 2 * N2)))
    for name in which:
        if name == "convolve":
            made = joined(
                mix_real * filter_real - mix_imaginary * filter_imaginary,
                mix_real * filter_imaginary + mix_imaginary * filter_real,
            )
        elif name == "correlate":
            made = joined(
                filter_real * weight_real + filter_imaginary * weight_imaginary,
                filter_real * weight_imaginary - filter_imaginary * weight_real,
            )
        else:
            made = joined(
                mix_real * weight_real + mix_imaginary * weight_imaginary,
                mix_real * weight_imaginary - mix_imaginary * weight_real,
            )
        outcome.append(made.reshape(lead + (-1, 2 * N2)))
    return outcome


def shards(input_gate, output_gate, values, cotangent, filter_raw, filter_decay, skip_gain):
    context_size = lax.axis_size("ctx")
    context_index = lax.axis_index("ctx")
    channels, local_len = input_gate.shape
    filters = filter_raw.shape[0]
    groups = channels // filters
    row_local = local_len // N2
    row_total = row_local * context_size
    seq_len = local_len * context_size
    first_forward, first_inverse = first_tables(row_total)
    second_forward, second_inverse = second_tables()
    inverse_scale = 1.0 / FFT_LEN
    mixed_input = (input_gate.astype(jnp.float32) * values.astype(jnp.float32)).astype(jnp.bfloat16)
    weighted = (cotangent.astype(jnp.float32) * output_gate.astype(jnp.float32)).astype(
        jnp.bfloat16
    )
    global_positions = (context_index * local_len + jnp.arange(local_len, dtype=jnp.int32)).astype(
        jnp.float32
    )
    envelope = jnp.exp(-filter_decay[:, None] * (global_positions[None, :] / seq_len))
    filter_scale = seq_len ** (-0.5)
    filter_taps = (filter_raw.astype(jnp.float32) * envelope * filter_scale).astype(jnp.bfloat16)
    spread_count = filters // context_size
    full_real, full_imaginary = twiddle_table(
        jnp.arange(N1, dtype=jnp.int32), jnp.arange(N2, dtype=jnp.int32)
    )
    pair = jnp.stack([mixed_input, weighted], axis=0).reshape(2, groups, filters, row_local, N2)
    taps_block = filter_taps.reshape(1, 1, filters, row_local, N2)
    pair_whole, taps_whole = (
        lax.all_to_all(pair, "ctx", split_axis=2, concat_axis=3, tiled=True),
        lax.all_to_all(taps_block, "ctx", split_axis=2, concat_axis=3, tiled=True),
    )
    signal_count = 2 * groups * spread_count
    every = jnp.concatenate(
        [
            pair_whole.reshape(signal_count, row_total, N2),
            taps_whole.reshape(spread_count, row_total, N2),
        ],
        axis=0,
    )
    first = jnp.einsum("km,imn->ikn", first_forward, every, preferred_element_type=jnp.float32)
    first_real = first[:, :N1]
    first_imaginary = first[:, N1:]
    turned = jnp.stack(
        [
            first_real * full_real - first_imaginary * full_imaginary,
            first_real * full_imaginary + first_imaginary * full_real,
        ],
        axis=1,
    ).astype(jnp.bfloat16)
    spectra = jnp.einsum(
        "ipkn,pnl->ikl", turned, second_forward, preferred_element_type=jnp.float32
    )
    signal_spec = spectra[:signal_count].reshape(2, groups * spread_count, N1, 2 * N2)
    filter_spec = spectra[signal_count:].astype(jnp.bfloat16)
    filter_spec = jnp.transpose(filter_spec, (1, 0, 2))
    mix_spec = jnp.transpose(signal_spec[0], (1, 0, 2))
    weight_spec = jnp.transpose(signal_spec[1], (1, 0, 2))
    made = spectral_products(mix_spec, weight_spec, filter_spec, ["convolve", "correlate", "lag"])
    stacked = jnp.transpose(jnp.concatenate(made, axis=1), (1, 0, 2))
    back = jnp.einsum("ikl,lm->ikm", stacked, second_inverse, preferred_element_type=jnp.float32)
    back_real, back_imaginary = halves(back)
    rotated = jnp.stack(
        [
            (back_real * full_real + back_imaginary * full_imaginary) * inverse_scale,
            (back_imaginary * full_real - back_real * full_imaginary) * inverse_scale,
        ],
        axis=1,
    ).astype(jnp.bfloat16)
    inverted = jnp.einsum(
        "mkp,ipkn->imn", first_inverse, rotated, preferred_element_type=jnp.float32
    )
    inverted = inverted.astype(jnp.bfloat16).reshape(3, groups, spread_count, row_total, N2)
    back_rows = lax.all_to_all(inverted[:2], "ctx", split_axis=3, concat_axis=2, tiled=True)
    convolved = back_rows[0].reshape(channels, local_len)
    correlated = back_rows[1].reshape(channels, local_len)
    lag_whole = jnp.sum(inverted[2].astype(jnp.float32), axis=0)
    lag_part = (
        lax.all_to_all(
            lag_whole.astype(jnp.bfloat16), "ctx", split_axis=1, concat_axis=0, tiled=True
        )
        .astype(lag_whole.dtype)
        .reshape(filters, local_len)
    )
    summed = convolved.astype(jnp.float32) + skip_gain[:, None] * mixed_input.astype(jnp.float32)
    outputs = (output_gate.astype(jnp.float32) * summed).astype(jnp.bfloat16)
    grad_output_gate = (cotangent.astype(jnp.float32) * summed).astype(jnp.bfloat16)
    back_total = correlated.astype(jnp.float32) + skip_gain[:, None] * weighted.astype(jnp.float32)
    grad_input_gate = (back_total * values.astype(jnp.float32)).astype(jnp.bfloat16)
    grad_values = (back_total * input_gate.astype(jnp.float32)).astype(jnp.bfloat16)
    lag_total = over_pieces(lag_part.astype(jnp.bfloat16), "dp").astype(jnp.float32)
    grad_filter = lag_total * envelope * filter_scale
    return (outputs, grad_input_gate, grad_output_gate, grad_values, grad_filter)


def solution(mesh):
    return jax.shard_map(
        shards,
        mesh=mesh,
        in_specs=(
            P("dp", "ctx"),
            P("dp", "ctx"),
            P("dp", "ctx"),
            P("dp", "ctx"),
            P(None, "ctx"),
            P(),
            P("dp"),
        ),
        out_specs=(P("dp", "ctx"), P("dp", "ctx"), P("dp", "ctx"), P("dp", "ctx"), P(None, "ctx")),
        check_vma=False,
    )
```

profile of v0, /device:TPU:1, one launch (start us, length us, event | category | flops | bytes accessed | tf_op | source)
XLA Modules:
  0.0 178.3 jit_solution(17833593253118888439)
XLA Ops:
  9.8 11.6 %all-to-all-start.1 = ((bf16[1,1,16,16,512]{4,3,1,0,2:T(8,128)(2,1)}), bf16[1,1,16,16,512]{4,3,1,0,2:T(8,128)(2,1)S(1)}, u32[]{:S(2)}, u32[]{:S(2)}) async-start(bf16[1,1,16,16,512]{4,3,1,0,2:T(8,128)(2,1)} %bitcast.48), calls=%async_computation.1 | async-start | bytes 524288 | tf_op jit(solution)/shard_map/all_to_all | solution.py:129
  21.4 1.8 fusion.44
  24.7 8.7 %all-to-all-done.1 = bf16[1,1,16,16,512]{4,3,1,0,2:T(8,128)(2,1)S(1)} async-done(((bf16[1,1,16,16,512]{4,3,1,0,2:T(8,128)(2,1)}), bf16[1,1,16,16,512]{4,3,1,0,2:T(8,128)(2,1)S(1)}, u32[]{:S(2)}, u32[]{:S(2)}) %all-to-all-start.1) | async-done | bytes 262176 | tf_op jit(solution)/shard_map/all_to_all | solution.py:129
  33.4 4.3 %all-to-all-start = ((bf16[2,2,16,16,512]{4,3,1,0,2:T(8,128)(2,1)}), bf16[2,2,16,16,512]{4,3,1,0,2:T(8,128)(2,1)}, u32[]{:S(2)}, u32[]{:S(2)}) async-start(bf16[2,2,16,16,512]{4,3,1,0,2:T(8,128)(2,1)} %copy.50), calls=%async_computation | async-start | bytes 2097152 | tf_op jit(solution)/shard_map/all_to_all | solution.py:128
  37.8 4.1 %sine_negate_fusion = (f32[512,512]{1,0:T(8,128)S(1)}, f32[512,512]{1,0:T(8,128)S(1)}) fusion(), kind=kLoop, calls=%fused_computation.93 | loop fusion | flops 3932160 | bytes 2097152 | tf_op jit(solution)/shard_map/neg | solution.py:59
  44.5 2.2 %negate_convert_fusion.2 = (bf16[512,256]{1,0:T(8,128)(2,1)S(1)}, bf16[512,256]{1,0:T(8,128)(2,1)S(1)}) fusion(), kind=kLoop, calls=%fused_computation.129 | loop fusion | flops 2228224 | bytes 524288 | tf_op jit(solution)/shard_map/convert_element_type | solution.py:25
  46.7 4.0 %fusion.84 = bf16[512,512]{1,0:T(8,128)(2,1)S(1)} fusion(), kind=kLoop, calls=%fused_computation.137 | loop fusion | flops 4980736 | bytes 524288 | tf_op jit(solution)/shard_map/neg | solution.py:41
  50.8 2.9 %negate_convert_fusion.1 = (bf16[256,512,1]{1,0,2:T(8,128)(2,1)}, bf16[256,512,1]{1,0,2:T(8,128)(2,1)}) fusion(), kind=kLoop, calls=%fused_computation.124 | loop fusion | flops 2228224 | bytes 524288 | tf_op jit(solution)/shard_map/convert_element_type | solution.py:25
  53.7 4.3 %negate_convert_fusion = (bf16[512,512]{1,0:T(8,128)(2,1)S(1)}, bf16[512,512]{1,0:T(8,128)(2,1)S(1)}) fusion(), kind=kLoop, calls=%fused_computation.91 | loop fusion | flops 4456448 | bytes 1048576 | tf_op jit(solution)/shard_map/convert_element_type | solution.py:37
  58.1 1.7 maximum_bitcast_fusion.6
  60.8 2.7 %all-to-all-done = bf16[2,2,16,16,512]{4,3,1,0,2:T(8,128)(2,1)} async-done(((bf16[2,2,16,16,512]{4,3,1,0,2:T(8,128)(2,1)}), bf16[2,2,16,16,512]{4,3,1,0,2:T(8,128)(2,1)}, u32[]{:S(2)}, u32[]{:S(2)}) %all-to-all-start) | async-done | bytes 1048608 | tf_op jit(solution)/shard_map/all_to_all | solution.py:128
  63.6 2.3 %copy.51 = bf16[2,2,16,16,512]{4,3,2,1,0:T(8,128)(2,1)} copy(bf16[2,2,16,16,512]{4,3,1,0,2:T(8,128)(2,1)} %all-to-all-done) | data formatting | bytes 2097152 | tf_op jit(solution)/shard_map/all_to_all | solution.py:128
  69.0 2.2 %fusion.24 = (bf16[5,1,512,512]{2,3,0,1:T(8,128)(2,1)S(1)}, bf16[5,1,512,512]{2,3,0,1:T(8,128)(2,1)S(1)}) fusion(f32[5,1024,512]{1,2,0:T(8,128)S(1)} %convolution_bitcast_fusion, f32[512,512]{0,1:T(8,128)S(1)} %copy-done.4, f32[512,512]{0,1:T(8,128)S(1)} %copy-done.3), kind=kLoop, calls=%fused_computation.32 | loop fusion | flops 10485760 | bytes 17825792 | tf_op jit(solution)/shard_map/stack | solution.py:142
  71.2 5.8 %fusion.19 = f32[5,512,1024]{2,1,0:T(8,128)S(1)} fusion(bf16[5,1,512,512]{2,3,0,1:T(8,128)(2,1)S(1)} %get-tuple-element.8, bf16[5,1,512,512]{2,3,0,1:T(8,128)(2,1)S(1)} %get-tuple-element.7, bf16[1,512,1024]{2,1,0:T(8,128)(2,1)S(1)} %copy-done.10, bf16[1,512,1024]{2,1,0:T(8,128)(2,1)S(1)} %copy-done.9), kind=kOutput, calls=%fused_computation.27 | convolution fusion | flops 5372379136 | bytes 17825792 | tf_op jit(solution)/shard_map/ipkn,pnl->ikl/dot_general | solution.py:149
  79.2 3.6 %fusion.52 = (bf16[512,2,512]{2,0,1:T(8,128)(2,1)}, bf16[512,2,512]{2,0,1:T(8,128)(2,1)}, bf16[512,2,512]{2,0,1:T(8,128)(2,1)}, bf16[512,2,512]{2,0,1:T(8,128)(2...) fusion(f32[512,2,1,1024]{3,0,1,2:T(8,128)S(1)} %get-tuple-element.9, ...), kind=kLoop, calls=%fused_computation.76 | loop fusion | flops 12582912 | bytes 16777216 | tf_op jit(solution)/shard_map/concatenate | solution.py:67
  82.8 10.1 %fusion = f32[6,512,1024]{2,1,0:T(8,128)S(1)} fusion(bf16[512,2,512]{2,0,1:T(8,128)(2,1)} %get-tuple-element.17, bf16[512,2,512]{2,0,1:T(8,128)(2,1)} %get-tuple-element.18, bf16[512,2,512]{2,0,1:T(8,128)(2,1)} %get-tuple-element.19, bf16[512,2,512]{2,0,1:T(8,128)(2,1)} %get-tuple-element.20, bf16[512,2,512]{2,0,1:T(8,128)(2,1)} %get-tuple-element.14, ...), kind=kOutput, calls=%fused_computation.2 | convolution fusion | flops 6488588288 | bytes 20447232 | tf_op jit(solution)/shard_map/ikl,lm->ikm/dot_general | solution.py:159
  92.9 3.2 %fusion.22 = (bf16[6,1,512,512]{3,2,0,1:T(8,128)(2,1)S(1)}, bf16[6,1,512,512]{3,2,0,1:T(8,128)(2,1)S(1)}) fusion(f32[6,512,1024]{2,1,0:T(8,128)S(1)} %fusion, f32[512,512]{1,0:T(8,128)S(1)} %get-tuple-element.37, f32[512,512]{1,0:T(8,128)} %copy-done), kind=kLoop, calls=%fused_computation.29 | loop fusion | flops 15728640 | bytes 20971520 | tf_op jit(solution)/shard_map/stack | solution.py:161
  96.1 2.4 %fusion.36 = bf16[6,256,512]{1,2,0:T(8,128)(2,1)S(1)} fusion(bf16[6,1,512,512]{3,2,0,1:T(8,128)(2,1)S(1)} %get-tuple-element.6, bf16[6,1,512,512]{3,2,0,1:T(8,128)(2,1)S(1)} %get-tuple-element.5, bf16[256,512,1]{1,0,2:T(8,128)(2,1)S(1)} %copy-done.12, bf16[256,512,1]{1,0,2:T(8,128)(2,1)S(1)} %copy-done.13), kind=kOutput, calls=%fused_computation.56 | convolution fusion | flops 1614807040 | bytes 8388608 | tf_op jit(solution)/shard_map/mkp,ipkn->imn/dot_general | solution.py:168
  99.6 2.2 %reduce.5 = bf16[256,512]{1,0:T(8,128)(2,1)S(1)} reduce(bf16[256,1,512]{2,1,0:T(2,128)(2,1)S(1)} %bitcast.95, bf16[]{:T(256)} %broadcast.205), dimensions={1}, to_apply=%bitcast.88.reduce_sub_computation | reduce | bytes 524290
  102.0 18.3 %all_to_all.19 = bf16[16,2,4096]{2,1,0:T(2,128)(2,1)S(1)} all-to-all(bf16[16,2,4096]{2,1,0:T(2,128)(2,1)S(1)} %reshape.268), channel_id=1, replica_groups=mesh['dp'=16,'ctx'=16] {'ctx'}, dimensions={0} | all-to-all | bytes 524288 | tf_op jit(solution)/shard_map/all_to_all | solution.py:177
  124.1 29.3 %all_to_all.40 = bf16[2,2,1,256,512]{4,1,0,2,3:T(2,128)(2,1)S(1)} all-to-all(bf16[2,2,1,256,512]{4,1,0,2,3:T(2,128)(2,1)S(1)} %copy.58), channel_id=1, replica_groups=mesh['dp'=16,'ctx'=16] {'ctx'}, dimensions={3} | all-to-all | bytes 2097152 | tf_op jit(solution)/shard_map/all_to_all | solution.py:172
  156.8 3.8 %fusion.43 = (bf16[32,8192]{1,0:T(8,128)(2,1)}, bf16[32,8192]{1,0:T(8,128)(2,1)}, bf16[32,8192]{1,0:T(8,128)(2,1)}, bf16[32,8192]{1,0:T(8,128)(2,1)}) fusion(bf16[32,8192]{1,0:T(8,128)(2,1)S(1)} %copy-done.8, f32[32,8192]{1,0:T(8,128)} %reshape.260, bf16[32,8192]{1,0:T(8,128)(2,1)S(1)} %copy-done.2, f32[32]{0:T(128)S(1)} %copy-done.14, ...), kind=kLoop, calls=%fused_computation.67 | loop fusion | flops 4718592 | bytes 7340160 | tf_op jit(solution)/shard_map/convert_element_type | solution.py:188
  160.7 7.0 %all-gather.2.cloned.1.call-done = bf16[16,16,8192]{2,1,0:T(8,128)(2,1)} async-done(((bf16[1,16,8192]{2,1,0:T(8,128)(2,1)}), bf16[16,16,8192]{2,1,0:T(8,128)(2,1)}) %all-gather.2.cloned.1.call-update) | async-done | bytes 4194320 | tf_op jit(solution)/shard_map/all_gather | solution.py:17
  167.6 2.8 %convert_reduce_fusion = f32[16,8192]{1,0:T(8,128)S(1)} fusion(bf16[16,16,8192]{2,1,0:T(8,128)(2,1)} %all-gather.2.cloned.1.call-done), kind=kLoop, calls=%fused_computation | loop fusion | flops 4063232 | bytes 4718592 | tf_op jit(solution)/shard_map/reduce_sum | solution.py:17
  (63 shorter events, 22.3 us)
Async XLA Ops:
  9.8 23.6 %all-to-all-start.1 = ((bf16[1,1,16,16,512]{4,3,1,0,2:T(8,128)(2,1)}), bf16[1,1,16,16,512]{4,3,1,0,2:T(8,128)(2,1)S(1)}, u32[]{:S(2)}, u32[]{:S(2)}) async-start(bf16[1,1,16,16,512]{4,3,1,0,2:T(8,128)(2,1)} %bitcast.48), calls=%async_computation.1 | async-start | bytes 524288 | tf_op jit(solution)/shard_map/all_to_all | solution.py:129
  23.1 10.2 %copy-start.1 = (bf16[32,8192]{1,0:T(8,128)(2,1)}, bf16[32,8192]{1,0:T(8,128)(2,1)S(1)}, u32[]{:S(2)}) copy-start(bf16[32,8192]{1,0:T(8,128)(2,1)S(1)} %get-tuple-element.42) | copy-start | bytes 1572868
  33.4 11.2 %copy-start.11 = (bf16[1,1,16,16,512]{4,3,1,0,2:T(8,128)(2,1)}, bf16[1,1,16,16,512]{4,3,1,0,2:T(8,128)(2,1)S(1)}, u32[]{:S(2)}) copy-start(bf16[1,1,16,16,512]{4,3,1,0,2:T(8,128)(2,1)S(1)} %all-to-all-done.1) | copy-start | bytes 786436
  33.4 30.2 %all-to-all-start = ((bf16[2,2,16,16,512]{4,3,1,0,2:T(8,128)(2,1)}), bf16[2,2,16,16,512]{4,3,1,0,2:T(8,128)(2,1)}, u32[]{:S(2)}, u32[]{:S(2)}) async-start(bf16[2,2,16,16,512]{4,3,1,0,2:T(8,128)(2,1)} %copy.50), calls=%async_computation | async-start | bytes 2097152 | tf_op jit(solution)/shard_map/all_to_all | solution.py:128
  37.7 129.9 %all-gather.2.cloned.1.call-start = ((), (), s32[]{:S(2)}) async-start(), calls=%async_computation.4 | async-start | bytes 4456448 | tf_op jit(solution)/shard_map/all_gather | solution.py:17
  41.9 17.9 %copy-start = (f32[512,512]{1,0:T(8,128)}, f32[512,512]{1,0:T(8,128)S(1)}, u32[]{:S(2)}) copy-start(f32[512,512]{1,0:T(8,128)S(1)} %get-tuple-element.38) | copy-start | bytes 3145732
  50.8 7.3 %copy-start.5 = (bf16[512,512]{1,0:T(8,128)(2,1)}, bf16[512,512]{1,0:T(8,128)(2,1)S(1)}, u32[]{:S(2)}) copy-start(bf16[512,512]{1,0:T(8,128)(2,1)S(1)} %fusion.84) | copy-start | bytes 1572868
  58.0 1.7 copy-start.6
  58.1 1.7 copy-start.7
  67.3 1.6 copy-start.3
  67.3 1.6 copy-start.4
  68.9 2.3 %copy-start.9 = (bf16[1,512,1024]{2,1,0:T(8,128)(2,1)S(1)}, bf16[1,512,1024]{2,1,0:T(8,128)(2,1)}, u32[]{:S(2)}) copy-start(bf16[1,512,1024]{2,1,0:T(8,128)(2,1)} %get-tuple-element.29) | copy-start | bytes 3145732
  68.9 2.3 %copy-start.10 = (bf16[1,512,1024]{2,1,0:T(8,128)(2,1)S(1)}, bf16[1,512,1024]{2,1,0:T(8,128)(2,1)}, u32[]{:S(2)}) copy-start(bf16[1,512,1024]{2,1,0:T(8,128)(2,1)} %get-tuple-element.30) | copy-start | bytes 3145732
  92.9 3.2 %copy-start.12 = (bf16[256,512,1]{1,0,2:T(8,128)(2,1)S(1)}, bf16[256,512,1]{1,0,2:T(8,128)(2,1)}, u32[]{:S(2)}) copy-start(bf16[256,512,1]{1,0,2:T(8,128)(2,1)} %get-tuple-element.39) | copy-start | bytes 786436
  92.9 3.2 %copy-start.13 = (bf16[256,512,1]{1,0,2:T(8,128)(2,1)S(1)}, bf16[256,512,1]{1,0,2:T(8,128)(2,1)}, u32[]{:S(2)}) copy-start(bf16[256,512,1]{1,0,2:T(8,128)(2,1)} %get-tuple-element.40) | copy-start | bytes 786436
  154.1 2.7 %copy-start.2 = (bf16[32,8192]{1,0:T(8,128)(2,1)S(1)}, bf16[32,8192]{1,0:T(8,128)(2,1)}, u32[]{:S(2)}) copy-start(bf16[32,8192]{1,0:T(8,128)(2,1)} %copy-done.1) | copy-start | bytes 1572868
  154.2 2.7 %copy-start.8 = (bf16[32,8192]{1,0:T(8,128)(2,1)S(1)}, bf16[32,8192]{1,0:T(8,128)(2,1)}, u32[]{:S(2)}) copy-start(bf16[32,8192]{1,0:T(8,128)(2,1)} %param.7) | copy-start | bytes 1572868
  154.2 2.7 %copy-start.14 = (f32[32]{0:T(128)S(1)}, f32[32]{0:T(128)}, u32[]{:S(2)}) copy-start(f32[32]{0:T(128)} %param.13) | copy-start | bytes 388
Sparse Core Ops, SparseCore 0:
  123.0 44.5 all-gather.1
where the time goes:
time: 179 us; the launch traced here: 178 us
  blocking collectives  47.6 us (27%)
  other arithmetic  42.3 us (24%)
  matrix products  19.9 us (11%)
  local copies, waits for them, and re-layouts  19.6 us (11%)
  waiting for transfers between devices  18.4 us (10%)
  starting transfers between devices  16 us (9%)
  between operations  14.5 us (8%)
    all_to_all x1, blocking collectives, shards(): lax.all_to_all(inverted[:2], 'ctx', split_axis=3, concat_axis=2, tiled=True)  29.3 us
    all_to_all x1, blocking collectives, shards(): lax.all_to_all(lag_whole.astype(jnp.bfloat16), 'ctx', split_axis=1, conca...  18.3 us
    all_to_all x1, starting transfers between devices, shards(): lax.all_to_all(taps_block, 'ctx', split_axis=2, concat_axis=3, tiled=True)  11.6 us
    dot_general x1, matrix products, shards(): jnp.einsum('ikl,lm->ikm', stacked, second_inverse, preferred_element_type...  10.1 us
    all_to_all x1, waiting for transfers between devices, shards(): lax.all_to_all(taps_block, 'ctx', split_axis=2, concat_axis=3, tiled=True)  8.7 us
    all_gather x1, waiting for transfers between devices, over_pieces(): return lax.all_gather(x, axis).astype(jnp.float32).sum(0)  6.99 us
    dot_general x1, matrix products, shards(): jnp.einsum('ipkn,pnl->ikl', turned, second_forward, preferred_element_typ...  5.84 us
    convert_element_type x2, other arithmetic, first_tables(): minus_sine = (-jnp.sin(angles)).astype(jnp.bfloat16)  5.11 us
  transfers between devices with their start and end apart: 3, of which 3 were waited for; matrix products, arithmetic and copies ran while one was open for 19% of the time, Pallas kernels for 0%

commit v1 on v0

v1 whole, which is shorter than its diff:
```python
import functools

import jax
import jax.numpy as jnp
import numpy as np
from jax import lax
from jax.experimental import pallas as pl
from jax.experimental.pallas import tpu as pltpu
from jax.sharding import PartitionSpec as P

N = 512
FFT_LEN = N * N
SEQ = FFT_LEN // 2
CTX = 16
ROWS = 16
LOCAL = ROWS * N
HALF = N // 2
QUARTER = N // 4
SCALE = SEQ**-0.5
CHUNK = 256
MESH = pl.DeviceIdType.MESH
F32 = jnp.float32
BF16 = jnp.bfloat16


def constant_tables():
    index = np.arange(N)
    angle = (index[:, None] * index[None, :] % N) * (2.0 * np.pi / N)
    roots = np.stack([np.cos(angle), np.sin(angle)]).astype(jnp.bfloat16)
    coarse = np.arange(N // ROWS)[:, None] * ROWS * index[None, :] * (2.0 * np.pi / FFT_LEN)
    fine = np.arange(ROWS)[:, None] * index[None, :] * (2.0 * np.pi / FFT_LEN)
    both = np.concatenate([coarse, fine], axis=0)
    turns = np.stack([np.cos(both), -np.sin(both)]).astype(np.float32)
    return roots, turns


def dot(left, right):
    return jnp.dot(left, right, preferred_element_type=F32)


def times(ar, ai, br, bi):
    return ar * br - ai * bi, ar * bi + ai * br


def conj_times(ar, ai, br, bi):
    return ar * br + ai * bi, ar * bi - ai * br


def joined(real, imaginary):
    return jnp.concatenate([real, imaginary], axis=1).astype(BF16)


def parts(value):
    return value[:, :N], value[:, N:]


def step_of(i):
    j = i // 2
    return 4 + (1 - 2 * (j % 2)) * ((j + 1) // 2), 1 - i % 2


def kernel(
    ig_hbm, va_hbm, ct_hbm, og_hbm, fr_hbm, decay_hbm, skip_hbm, roots_hbm, turns_hbm,
    out_hbm, gig_hbm, gog_hbm, gva_hbm, gf_hbm,
    ig, va, ct, og, fr, decay, skip, roots, turns,
    out, gig, gog, gva, gf,
    first, first_back, second, second_back, wr, wi, perm,
    mixed, weighted, send_m, recv_m, send_w, recv_w,
    send_t, taps_q, taps, spec_h, spec_m, turned, turned_lag,
    send_c, recv_c, send_u, recv_u, summed,
    lag_q, lag_y, lag_z, lag_f, lag_x, lag_g, lag,
    in_sem, out_sem, ctx_send, ctx_recv, dp_send, dp_recv,
):
    dp = lax.axis_index("dp")
    me = lax.axis_index("ctx")
    my_z, my_x = me // 2, me % 2
    low, my_y, core = dp // 8, (dp // 2) % 4, dp % 2

    def ctx_peer(i):
        dz, dx = step_of(i)
        return ((my_z + dz) % 8) * 2 + (my_x + dx) % 2

    def y_peer(j):
        y = (my_y + 1 + j) % 4
        return y, low * 8 + y * 2 + core

    def side_peer(j):
        flip = j + 1
        other_low = (low + flip // 2) % 2
        other_core = (core + flip % 2) % 2
        return other_low * 8 + my_y * 2 + other_core

    barrier = pltpu.get_barrier_semaphore()

    def greet(i, carry):
        pl.semaphore_signal(barrier, inc=1, device_id={"ctx": ctx_peer(i)}, device_id_type=MESH)
        return carry

    lax.fori_loop(0, CTX - 1, greet, 0)
    for j in range(3):
        pl.semaphore_signal(barrier, inc=1, device_id={"dp": y_peer(j)[1]}, device_id_type=MESH)
        pl.semaphore_signal(barrier, inc=1, device_id={"dp": side_peer(j)}, device_id_type=MESH)

    loads = [
        pltpu.make_async_copy(source, target, in_sem.at[i])
        for i, (source, target) in enumerate(
            [
                (decay_hbm, decay), (fr_hbm, fr), (ig_hbm, ig), (va_hbm, va), (ct_hbm, ct),
                (og_hbm, og), (roots_hbm, roots), (turns_hbm, turns), (skip_hbm, skip),
            ]
        )
    ]
    for load in loads:
        load.start()

    row = lax.broadcasted_iota(jnp.int32, (256, 256), 0)
    col = lax.broadcasted_iota(jnp.int32, (256, 256), 1)
    perm[...] = jnp.where(col == (row % 16) * 16 + row // 16, 1.0, 0.0).astype(BF16)

    def column(line, count):
        r = lax.broadcasted_iota(jnp.int32, (count, count), 0)
        c = lax.broadcasted_iota(jnp.int32, (count, count), 1)
        return jnp.sum(jnp.where(r == c, line, 0.0), axis=1, keepdims=True)

    loads[0].wait()
    loads[1].wait()
    decay_column = column(decay[...], 16)

    def envelope(start, width):
        place = start + lax.broadcasted_iota(jnp.int32, (16, width), 1)
        place = (me * LOCAL + place).astype(F32)
        return jnp.exp(-decay_column * (place * (1.0 / SEQ)))

    def taps_row(r, carry):
        start = pl.multiple_of(r * N + my_y * QUARTER, QUARTER)
        raw = fr[:, pl.ds(start, QUARTER)].astype(F32)
        made = (raw * envelope(start, QUARTER) * SCALE).astype(BF16)
        turned[pl.ds(pl.multiple_of(r * 16, 16), 16), 0:QUARTER] = made
        return carry

    lax.fori_loop(0, ROWS, taps_row, 0)
    send_t[...] = dot(perm[...], turned[0:256, 0:QUARTER]).astype(BF16)

    def multiply(left, right, target, send):
        for g in range(2):

            def block(r, carry, g=g):
                lanes = pl.ds(pl.multiple_of(r * N, N), N)
                a = left[g * 16 : g * 16 + 16, lanes].astype(F32)
                b = right[g * 16 : g * 16 + 16, lanes].astype(F32)
                target[g, pl.ds(pl.multiple_of(r * 16, 16), 16), :] = (a * b).astype(BF16)
                return carry

            lax.fori_loop(0, ROWS, block, 0)
            send[g] = dot(perm[...], target[g]).astype(BF16).reshape(16, 16, N)

    def exchange(k, send, recv):
        def copy(i):
            return pltpu.make_async_remote_copy(
                src_ref=send.at[:, ctx_peer(i)],
                dst_ref=recv.at[:, me],
                send_sem=ctx_send.at[k, i],
                recv_sem=ctx_recv.at[k, i],
                device_id={"ctx": ctx_peer(i)},
                device_id_type=MESH,
            )

        return copy

    def small_exchange(k, send, recv):
        def copy(i):
            return pltpu.make_async_remote_copy(
                src_ref=send.at[pl.ds(pl.multiple_of(ctx_peer(i) * 16, 16), 16), :],
                dst_ref=recv.at[pl.ds(pl.multiple_of(me * 16, 16), 16), :],
                send_sem=ctx_send.at[k, i],
                recv_sem=ctx_recv.at[k, i],
                device_id={"ctx": ctx_peer(i)},
                device_id_type=MESH,
            )

        return copy

    def over(copy, action, count=CTX - 1):
        def one(i, carry):
            getattr(copy(i), action)()
            return carry

        lax.fori_loop(0, count, one, 0)

    def keep(send, recv):
        recv[:, pl.ds(me, 1)] = send[:, pl.ds(me, 1)]

    def keep_small(send, recv):
        rows = pl.ds(pl.multiple_of(me * 16, 16), 16)
        recv[rows, :] = send[rows, :]

    loads[2].wait()
    loads[3].wait()
    pl.semaphore_wait(barrier, CTX - 1 + 6)
    copy_t = small_exchange(0, send_t, taps_q.at[my_y])
    over(copy_t, "start")
    multiply(ig, va, mixed, send_m)
    copy_m = exchange(1, send_m, recv_m)
    over(copy_m, "start")
    loads[4].wait()
    loads[5].wait()
    multiply(ct, og, weighted, send_w)
    copy_w = exchange(2, send_w, recv_w)
    over(copy_w, "start")
    keep_small(send_t, taps_q.at[my_y])
    keep(send_m, recv_m)
    keep(send_w, recv_w)

    loads[6].wait()
    loads[7].wait()
    loads[8].wait()
    cosine, sine = roots[0], roots[1]
    first[0:N, 0:HALF] = cosine[:, 0:HALF]
    first[0:N, HALF:N] = sine[:, 0:HALF]
    first[N:, 0:HALF] = -sine[:, 0:HALF]
    first[N:, HALF:N] = cosine[:, 0:HALF]
    first_back[0:HALF, 0:N] = cosine[0:HALF]
    first_back[0:HALF, N:] = -sine[0:HALF]
    first_back[HALF:, 0:N] = sine[0:HALF]
    first_back[HALF:, N:] = cosine[0:HALF]
    second[0:N, 0:N] = cosine
    second[0:N, N:] = -sine
    second[N:, 0:N] = sine
    second[N:, N:] = cosine
    second_back[0:N, 0:N] = cosine
    second_back[0:N, N:] = sine
    second_back[N:, 0:N] = -sine
    second_back[N:, N:] = cosine
    fine_r, fine_i = turns[0, 32:48, :], turns[1, 32:48, :]

    def turn_rows(a, carry):
        rows = pl.ds(pl.multiple_of(a * 16, 16), 16)
        tr, ti = times(turns[0, pl.ds(a, 1), :], turns[1, pl.ds(a, 1), :], fine_r, fine_i)
        wr[rows, :] = tr
        wi[rows, :] = ti
        return carry

    lax.fori_loop(0, N // 16, turn_rows, 0)

    over(copy_t, "wait_recv")

    def share_t(j):
        return pltpu.make_async_remote_copy(
            src_ref=taps_q.at[my_y],
            dst_ref=taps_q.at[my_y],
            send_sem=dp_send.at[0, j],
            recv_sem=dp_recv.at[0, j],
            device_id={"dp": y_peer(j)[1]},
            device_id_type=MESH,
        )

    over(share_t, "start", 3)
    over(share_t, "wait_recv", 3)
    for q in range(4):
        taps[:, q * QUARTER : (q + 1) * QUARTER] = taps_q[q]

    def forward(start, width, block):
        rows = pl.ds(start, CHUNK)
        pr = dot(first[rows, 0:width], block)
        pi = dot(first[pl.ds(start + N, CHUNK), 0:width], block)
        return dot(joined(*times(pr, pi, wr[rows, :], wi[rows, :])), second[...])

    def backward(start, spectrum, target):
        rows = pl.ds(start, CHUNK)
        br, bi = parts(dot(spectrum, second_back[...]))
        sr, si = conj_times(wr[rows, :], wi[rows, :], br, bi)
        target[rows, :] = (sr * (1.0 / FFT_LEN)).astype(BF16)
        target[pl.ds(start + N, CHUNK), :] = (si * (1.0 / FFT_LEN)).astype(BF16)

    def chunks(body):
        def one(i, carry):
            body(pl.multiple_of(i * CHUNK, CHUNK))
            return carry

        lax.fori_loop(0, N // CHUNK, one, 0)

    def filter_chunk(start):
        spec_h[pl.ds(start, CHUNK), :] = forward(start, HALF, taps[...]).astype(BF16)

    chunks(filter_chunk)

    over(copy_m, "wait_recv")

    def mix_chunk(start):
        rows = pl.ds(start, CHUNK)
        spectrum = forward(start, N, recv_m[...].reshape(N, N))
        spec_m[rows, :] = spectrum
        hr, hi = parts(spec_h[rows, :].astype(F32))
        backward(start, joined(*times(*parts(spectrum), hr, hi)), turned)

    chunks(mix_chunk)
    for g in range(2):
        made = dot(first_back[g * HALF : (g + 1) * HALF, :], turned[...])
        send_c[g] = made.astype(BF16).reshape(16, 16, N)
    copy_c = exchange(3, send_c, recv_c)
    over(copy_c, "start")
    keep(send_c, recv_c)

    over(copy_w, "wait_recv")

    def weight_chunk(start):
        rows = pl.ds(start, CHUNK)
        spectrum = parts(forward(start, N, recv_w[...].reshape(N, N)))
        hr, hi = parts(spec_h[rows, :].astype(F32))
        backward(start, joined(*conj_times(hr, hi, *spectrum)), turned)
        mr, mi = parts(spec_m[rows, :])
        backward(start, joined(*conj_times(mr, mi, *spectrum)), turned_lag)

    chunks(weight_chunk)
    lagged = dot(first_back[0:HALF, :], turned_lag[...]).astype(BF16)
    for q in range(4):
        lag_q[q] = lagged[:, q * QUARTER : (q + 1) * QUARTER]

    def scatter_y(j):
        y, device = y_peer(j)
        return pltpu.make_async_remote_copy(
            src_ref=lag_q.at[y],
            dst_ref=lag_y.at[my_y],
            send_sem=dp_send.at[1, j],
            recv_sem=dp_recv.at[1, j],
            device_id={"dp": device},
            device_id_type=MESH,
        )

    over(scatter_y, "start", 3)
    lag_y[pl.ds(my_y, 1)] = lag_q[pl.ds(my_y, 1)]
    for g in range(2):
        made = dot(first_back[g * HALF : (g + 1) * HALF, :], turned[...])
        send_u[g] = made.astype(BF16).reshape(16, 16, N)
    over(scatter_y, "wait_recv", 3)
    lag_z[...] = sum(lag_y[y].astype(F32) for y in range(4)).astype(BF16)
    copy_z = small_exchange(4, lag_z, lag_f)
    over(copy_z, "start")
    copy_u = exchange(5, send_u, recv_u)
    over(copy_u, "start")
    keep_small(lag_z, lag_f)
    keep(send_u, recv_u)

    skip_column = column(skip[...], 32)

    def finish(recv, base, left, right, first_out, second_out):
        for g in range(2):
            gain = skip_column[g * 16 : g * 16 + 16]
            summed[...] = dot(perm[...], recv[g].reshape(256, N))

            def block(r, carry, g=g, gain=gain):
                rows = pl.ds(pl.multiple_of(r * 16, 16), 16)
                lanes = pl.ds(pl.multiple_of(r * N, N), N)
                total = summed[rows, :] + gain * base[g, rows, :].astype(F32)
                place = slice(g * 16, g * 16 + 16)
                first_out[place, lanes] = (left[place, lanes].astype(F32) * total).astype(BF16)
                second_out[place, lanes] = (right[place, lanes].astype(F32) * total).astype(BF16)
                return carry

            lax.fori_loop(0, ROWS, block, 0)

    over(copy_z, "wait_recv")

    def share_side(j):
        return pltpu.make_async_remote_copy(
            src_ref=lag_f,
            dst_ref=lag_x.at[j],
            send_sem=dp_send.at[2, j],
            recv_sem=dp_recv.at[2, j],
            device_id={"dp": side_peer(j)},
            device_id_type=MESH,
        )

    over(share_side, "start", 3)
    over(copy_c, "wait_recv")
    finish(recv_c, mixed, og, ct, out, gog)
    stores = [
        pltpu.make_async_copy(source, target, out_sem.at[i])
        for i, (source, target) in enumerate(
            [(out, out_hbm), (gog, gog_hbm), (gf, gf_hbm), (gig, gig_hbm), (gva, gva_hbm)]
        )
    ]
    stores[0].start()
    stores[1].start()
    over(share_side, "wait_recv", 3)
    total = lag_f[...].astype(F32)
    for j in range(3):
        total = total + lag_x[j].astype(F32)
    lag_g[pl.ds(my_y, 1)] = total.astype(BF16)[None]

    def gather_y(j):
        return pltpu.make_async_remote_copy(
            src_ref=lag_g.at[my_y],
            dst_ref=lag_g.at[my_y],
            send_sem=dp_send.at[3, j],
            recv_sem=dp_recv.at[3, j],
            device_id={"dp": y_peer(j)[1]},
            device_id_type=MESH,
        )

    over(gather_y, "start", 3)
    over(gather_y, "wait_recv", 3)
    for q in range(4):
        lag[:, q * QUARTER : (q + 1) * QUARTER] = lag_g[q]
    summed[...] = dot(perm[...], lag[...])

    def filter_row(r, carry):
        start = pl.multiple_of(r * N, N)
        piece = summed[pl.ds(pl.multiple_of(r * 16, 16), 16), :]
        gf[:, pl.ds(start, N)] = piece * envelope(start, N) * SCALE
        return carry

    lax.fori_loop(0, ROWS, filter_row, 0)
    stores[2].start()
    over(copy_u, "wait_recv")
    finish(recv_u, weighted, va, ig, gig, gva)
    stores[3].start()
    stores[4].start()
    for copy in (copy_t, copy_m, copy_w, copy_c, copy_z, copy_u):
        over(copy, "wait_send")
    for copy in (share_t, scatter_y, share_side, gather_y):
        over(copy, "wait_send", 3)
    for store in stores:
        store.wait()


def shards(input_gate, output_gate, values, cotangent, filter_raw, filter_decay, skip_gain):
    roots, turns = constant_tables()
    signal = pltpu.VMEM((32, LOCAL), BF16)
    blocks = pltpu.VMEM((2, CTX, ROWS, N), BF16)
    quarter = pltpu.VMEM((256, QUARTER), BF16)
    quarters = pltpu.VMEM((4, 256, QUARTER), BF16)
    big = jax.ShapeDtypeStruct((32, LOCAL), BF16)
    anywhere = pl.BlockSpec(memory_space=pl.ANY)
    outputs, grad_input_gate, grad_output_gate, grad_values, grad_filter = pl.pallas_call(
        kernel,
        out_shape=(big, big, big, big, jax.ShapeDtypeStruct((16, LOCAL), F32)),
        in_specs=[anywhere] * 9,
        out_specs=(anywhere,) * 5,
        scratch_shapes=[
            signal, signal, signal, signal,
            pltpu.VMEM((16, LOCAL), BF16),
            pltpu.VMEM((1, 16), F32),
            pltpu.VMEM((1, 32), F32),
            pltpu.VMEM((2, N, N), BF16),
            pltpu.VMEM((2, 48, N), F32),
            signal, signal, signal, signal,
            pltpu.VMEM((16, LOCAL), F32),
            pltpu.VMEM((2 * N, N), BF16),
            pltpu.VMEM((N, 2 * N), BF16),
            pltpu.VMEM((2 * N, 2 * N), BF16),
            pltpu.VMEM((2 * N, 2 * N), BF16),
            pltpu.VMEM((N, N), F32),
            pltpu.VMEM((N, N), F32),
            pltpu.VMEM((256, 256), BF16),
            pltpu.VMEM((2, 256, N), BF16),
            pltpu.VMEM((2, 256, N), BF16),
            blocks, blocks, blocks, blocks,
            quarter,
            quarters,
            pltpu.VMEM((256, N), BF16),
            pltpu.VMEM((N, 2 * N), BF16),
            pltpu.VMEM((N, 2 * N), F32),
            pltpu.VMEM((2 * N, N), BF16),
            pltpu.VMEM((2 * N, N), BF16),
            blocks, blocks, blocks, blocks,
            pltpu.VMEM((256, N), F32),
            quarters,
            quarters,
            quarter,
            quarter,
            pltpu.VMEM((3, 256, QUARTER), BF16),
            quarters,
            pltpu.VMEM((256, N), BF16),
            pltpu.SemaphoreType.DMA((9,)),
            pltpu.SemaphoreType.DMA((5,)),
            pltpu.SemaphoreType.DMA((6, CTX - 1)),
            pltpu.SemaphoreType.DMA((6, CTX - 1)),
            pltpu.SemaphoreType.DMA((4, 3)),
            pltpu.SemaphoreType.DMA((4, 3)),
        ],
        compiler_params=pltpu.CompilerParams(
            collective_id=0, has_side_effects=True, vmem_limit_bytes=60 << 20
        ),
    )(
        input_gate, values, cotangent, output_gate, filter_raw,
        filter_decay.reshape(1, 16), skip_gain.reshape(1, 32), jnp.asarray(roots), jnp.asarray(turns),
    )
    return outputs, grad_input_gate, grad_output_gate, grad_values, grad_filter


def solution(mesh):
    return jax.shard_map(
        shards,
        mesh=mesh,
        in_specs=(
            P("dp", "ctx"),
            P("dp", "ctx"),
            P("dp", "ctx"),
            P("dp", "ctx"),
            P(None, "ctx"),
            P(),
            P("dp"),
        ),
        out_specs=(P("dp", "ctx"), P("dp", "ctx"), P("dp", "ctx"), P("dp", "ctx"), P(None, "ctx")),
        check_vma=False,
    )
```

time: 179 us -> 79.3 us (0.44)
  Pallas kernels: 0 us -> 71.7 us
  blocking collectives: 47.6 us -> 0 us
  other arithmetic: 42.3 us -> 0 us
  matrix products: 19.9 us -> 0 us
  waiting for transfers between devices: 18.4 us -> 0 us
  starting transfers between devices: 16 us -> 0 us
  between operations: 14.5 us -> 0.66 us
  local copies, waits for them, and re-layouts: 19.6 us -> 6.41 us
    pallas_call x0 -> x1, Pallas kernels: none -> 71.7 us  [shards(): pl.pallas_call(kernel, out_shape=(big, big, big, big, jax.ShapeDtypeStruc...]
    all_to_all x2 -> x0, blocking collectives: 47.6 us -> none  [the longest x1 29.3 us: shards(): lax.all_to_all(inverted[:2], 'ctx', split_axis=3, concat_axis=2, tiled=True)]
    dot_general x4 -> x0, matrix products: 19.9 us -> none  [the longest x1 10.1 us: shards(): jnp.einsum('ikl,lm->ikm', stacked, second_inverse, preferred_element_type...]
    convert_element_type x9 -> x0, other arithmetic: 16.7 us -> none  [the longest x2 5.11 us: first_tables(): minus_sine = (-jnp.sin(angles)).astype(jnp.bfloat16)]
    all_to_all x2 -> x0, starting transfers between devices: 15.9 us -> none  [the longest x1 11.6 us: shards(): lax.all_to_all(taps_block, 'ctx', split_axis=2, concat_axis=3, tiled=True)]
    all_to_all x2 -> x0, waiting for transfers between devices: 11.4 us -> none  [the longest x1 8.7 us: shards(): lax.all_to_all(taps_block, 'ctx', split_axis=2, concat_axis=3, tiled=True)]
    neg x3 -> x0, other arithmetic: 8.82 us -> none  [the longest x1 4.12 us: twiddle_table(): return (jnp.cos(angles), -jnp.sin(angles))]
    another operation x4 -> x0, other arithmetic: 7.21 us -> none  [the longest x1 3.2 us: shards(): jnp.stack([(back_real * full_real + back_imaginary * full_imaginary) * in...]
  transfers between devices with their start and end apart: 3 -> 0, of which waited for: 3 -> 0; matrix products, arithmetic and copies ran while one was open for 19% -> 0% of each run, Pallas kernels for 0% -> 0%
where the time goes in v1:
time: 79.3 us; the launch traced here: 78.8 us
  Pallas kernels  71.7 us (90%)
  local copies, waits for them, and re-layouts  6.41 us (8%)
    pallas_call x1, Pallas kernels, shards(): pl.pallas_call(kernel, out_shape=(big, big, big, big, jax.ShapeDtypeStruc...  71.7 us
    unnamed x13, local copies, waits for them, and re-layouts  6.41 us

profile of v1, /device:TPU:1, one launch (start us, length us, event | category | flops | bytes accessed | tf_op | source)
XLA Modules:
  0.0 78.8 jit_solution(6979002889310463176)
XLA Ops:
  0.6 71.7 %shard_map.128 = (bf16[32,8192]{1,0:T(8,128)(2,1)}, bf16[32,8192]{1,0:T(8,128)(2,1)}, bf16[32,8192]{1,0:T(8,128)(2,1)}, bf16[32,8192]{1,0:T(8,128)(2,1)}, f32[16,8192]{1,0:T(8,128)}) custom-call(bf16[32,8192]{1,0:T(8,128)(2,1)} %ig_hbm.1, bf16[32,8192]{1,0:T(8,128)(2,1)} %va_hbm.1, bf16[32,8192]{1,0:T(8,128)(2,1)} %ct_hbm.1, bf16[32,8192]{1,0:T(8,128)(2,1)} %og_hbm.1, ...), custom_call_target="tpu_custom_call" | custom-call | tf_op jit(solution)/shard_map/pallas_call | solution.py:435
  72.4 0.0 copy-start.3
  72.4 1.9 %copy.19 = bf16[32,8192]{1,0:T(8,128)(2,1)} copy(bf16[32,8192]{1,0:T(8,128)(2,1)} %get-tuple-element.10) | data formatting | bytes 1048576
  74.3 0.0 copy-done.3
  74.3 0.0 copy-start.2
  74.3 0.8 %copy.20 = bf16[32,8192]{1,0:T(8,128)(2,1)} copy(bf16[32,8192]{1,0:T(8,128)(2,1)S(1)} %copy-done.3) | data formatting | bytes 1048576
  75.1 0.4 copy-done.2
  75.6 0.0 copy-start.1
  75.6 0.8 %copy.21 = bf16[32,8192]{1,0:T(8,128)(2,1)} copy(bf16[32,8192]{1,0:T(8,128)(2,1)S(1)} %copy-done.2) | data formatting | bytes 1048576
  76.4 0.4 copy-done.1
  76.8 0.0 copy-start
  76.8 0.8 %copy.22 = bf16[32,8192]{1,0:T(8,128)(2,1)} copy(bf16[32,8192]{1,0:T(8,128)(2,1)S(1)} %copy-done.1) | data formatting | bytes 1048576
  77.6 0.4 copy-done
  78.0 0.8 %copy.23 = f32[16,8192]{1,0:T(8,128)} copy(f32[16,8192]{1,0:T(8,128)S(1)} %copy-done) | data formatting | bytes 1048576
Async XLA Ops:
  72.4 1.9 %copy-start.3 = (bf16[32,8192]{1,0:T(8,128)(2,1)S(1)}, bf16[32,8192]{1,0:T(8,128)(2,1)}, u32[]{:S(2)}) copy-start(bf16[32,8192]{1,0:T(8,128)(2,1)} %get-tuple-element.11) | copy-start | bytes 1572868
  74.3 1.2 %copy-start.2 = (bf16[32,8192]{1,0:T(8,128)(2,1)S(1)}, bf16[32,8192]{1,0:T(8,128)(2,1)}, u32[]{:S(2)}) copy-start(bf16[32,8192]{1,0:T(8,128)(2,1)} %get-tuple-element.12) | copy-start | bytes 1572868
  75.6 1.2 %copy-start.1 = (bf16[32,8192]{1,0:T(8,128)(2,1)S(1)}, bf16[32,8192]{1,0:T(8,128)(2,1)}, u32[]{:S(2)}) copy-start(bf16[32,8192]{1,0:T(8,128)(2,1)} %get-tuple-element.13) | copy-start | bytes 1572868
  76.8 1.2 %copy-start = (f32[16,8192]{1,0:T(8,128)S(1)}, f32[16,8192]{1,0:T(8,128)}, u32[]{:S(2)}) copy-start(f32[16,8192]{1,0:T(8,128)} %get-tuple-element.14) | copy-start | bytes 1572868

commit v2 on v1

v2 whole, which is shorter than its diff:
```python
import functools

import jax
import jax.numpy as jnp
import numpy as np
from jax import lax
from jax.experimental import pallas as pl
from jax.experimental.pallas import tpu as pltpu
from jax.sharding import PartitionSpec as P

N = 512
FFT_LEN = N * N
SEQ = FFT_LEN // 2
CTX = 16
ROWS = 16
LOCAL = ROWS * N
HALF = N // 2
QUARTER = N // 4
SCALE = SEQ**-0.5
CHUNK = 512
MESH = pl.DeviceIdType.MESH
F32 = jnp.float32
BF16 = jnp.bfloat16


def constant_tables():
    index = np.arange(N)
    angle = (index[:, None] * index[None, :] % N) * (2.0 * np.pi / N)
    roots = np.stack([np.cos(angle), np.sin(angle)]).astype(jnp.bfloat16)
    coarse = np.arange(N // ROWS)[:, None] * ROWS * index[None, :] * (2.0 * np.pi / FFT_LEN)
    fine = np.arange(ROWS)[:, None] * index[None, :] * (2.0 * np.pi / FFT_LEN)
    both = np.concatenate([coarse, fine], axis=0)
    turns = np.stack([np.cos(both), -np.sin(both)]).astype(np.float32)
    return roots, turns


def dot(left, right):
    return jnp.dot(left, right, preferred_element_type=F32)


def times(ar, ai, br, bi):
    return ar * br - ai * bi, ar * bi + ai * br


def conj_times(ar, ai, br, bi):
    return ar * br + ai * bi, ar * bi - ai * br


def joined(real, imaginary):
    return jnp.concatenate([real, imaginary], axis=1).astype(BF16)


def parts(value):
    return value[:, :N], value[:, N:]


def step_of(i):
    j = i // 2
    return 4 + (1 - 2 * (j % 2)) * ((j + 1) // 2), 1 - i % 2


def kernel(
    ig_hbm, va_hbm, ct_hbm, og_hbm, fr_hbm, decay_hbm, skip_hbm, roots_hbm, turns_hbm,
    out, gig, gog, gva, gf,
    ig, va, ct, og, fr, decay, skip, roots, turns,
    first, first_back, first_lag, first_taps, second, second_back, wr, wi, perm,
    mixed, weighted, send_m, recv_m, send_w, recv_w,
    send_t, taps_q, taps, spec_h, spec_m, spec_w, turned, turned_lag,
    send_c, recv_c, send_u, recv_u, summed,
    lag_q, lag_y, lag_z, lag_f, lag_g, lag,
    in_sem, ctx_send, ctx_recv, dp_send, dp_recv, lag_send, lag_recv,
):
    dp = lax.axis_index("dp")
    me = lax.axis_index("ctx")
    my_z, my_x = me // 2, me % 2
    place = dp % 8
    low, my_y, core = dp // 8, (dp // 2) % 4, dp % 2

    def ctx_peer(i):
        dz, dx = step_of(i)
        return ((my_z + dz) % 8) * 2 + (my_x + dx) % 2

    def plane_peer(j):
        place = (my_y * 2 + core + 1 + j) % 8
        return place, low * 8 + place

    def any_peer(i):
        moved = ctx_peer(i % (CTX - 1)) - me
        return (low + (i + 1) // CTX) % 2, me + moved * (1 - i // (2 * CTX - 2))

    barrier = pltpu.get_barrier_semaphore()

    def greet(i, carry):
        side, other = any_peer(i)
        device = (side * 8 + dp % 8, other)
        pl.semaphore_signal(barrier, inc=1, device_id=device, device_id_type=MESH)
        return carry

    def greet_plane(j, carry):
        pl.semaphore_signal(
            barrier, inc=1, device_id={"dp": plane_peer(j)[1]}, device_id_type=MESH
        )
        return carry

    lax.fori_loop(0, 2 * CTX - 1, greet, 0)
    lax.fori_loop(0, 7, greet_plane, 0)

    loads = [
        pltpu.make_async_copy(source, target, in_sem.at[i])
        for i, (source, target) in enumerate(
            [
                (ig_hbm, ig), (va_hbm, va), (decay_hbm, decay), (fr_hbm, fr), (ct_hbm, ct),
                (og_hbm, og), (roots_hbm, roots), (turns_hbm, turns), (skip_hbm, skip),
            ]
        )
    ]
    for load in loads:
        load.start()

    def selection(shape, where):
        row = lax.broadcasted_iota(jnp.int32, shape, 0)
        col = lax.broadcasted_iota(jnp.int32, shape, 1)
        return jnp.where(where(row, col), 1.0, 0.0).astype(BF16)

    perm[...] = selection((256, 256), lambda i, j: j == (i % 16) * 16 + i // 16)

    def column(line, count):
        r = lax.broadcasted_iota(jnp.int32, (count, count), 0)
        c = lax.broadcasted_iota(jnp.int32, (count, count), 1)
        return jnp.sum(jnp.where(r == c, line, 0.0), axis=1, keepdims=True)

    def multiply(left, right, target, send):
        for g in range(2):

            def block(r, carry, g=g):
                lanes = pl.ds(pl.multiple_of(r * N, N), N)
                a = left[g * 16 : g * 16 + 16, lanes].astype(F32)
                b = right[g * 16 : g * 16 + 16, lanes].astype(F32)
                target[g, pl.ds(pl.multiple_of(r * 16, 16), 16), :] = (a * b).astype(BF16)
                return carry

            lax.fori_loop(0, ROWS, block, 0)
            send[g] = dot(perm[...], target[g]).astype(BF16).reshape(16, 16, N)

    def exchange(k, send, recv):
        def copy(i):
            return pltpu.make_async_remote_copy(
                src_ref=send.at[:, ctx_peer(i)],
                dst_ref=recv.at[:, me],
                send_sem=ctx_send.at[k, i],
                recv_sem=ctx_recv.at[k, i],
                device_id={"ctx": ctx_peer(i)},
                device_id_type=MESH,
            )

        return copy

    def among(k, send, recv):
        def copy(j):
            return pltpu.make_async_remote_copy(
                src_ref=send(j),
                dst_ref=recv.at[place],
                send_sem=dp_send.at[k, j],
                recv_sem=dp_recv.at[k, j],
                device_id={"dp": plane_peer(j)[1]},
                device_id_type=MESH,
            )

        return copy

    def half_exchange(k, g, send, recv):
        def copy(i):
            return pltpu.make_async_remote_copy(
                src_ref=send.at[g, ctx_peer(i)],
                dst_ref=recv.at[g, me],
                send_sem=ctx_send.at[k, i],
                recv_sem=ctx_recv.at[k, i],
                device_id={"ctx": ctx_peer(i)},
                device_id_type=MESH,
            )

        return copy

    def small_exchange(k, send, recv):
        def copy(i):
            return pltpu.make_async_remote_copy(
                src_ref=send.at[ctx_peer(i)],
                dst_ref=recv.at[me],
                send_sem=ctx_send.at[k, i],
                recv_sem=ctx_recv.at[k, i],
                device_id={"ctx": ctx_peer(i)},
                device_id_type=MESH,
            )

        return copy

    def over(copy, action, count=CTX - 1, begin=0):
        def one(i, carry):
            getattr(copy(i), action)()
            return carry

        lax.fori_loop(begin, count, one, 0)

    def keep(send, recv):
        recv[:, pl.ds(me, 1)] = send[:, pl.ds(me, 1)]

    loads[2].wait()
    loads[3].wait()
    decay_column = column(decay[...], 16)

    def envelope(start, width):
        place = start + lax.broadcasted_iota(jnp.int32, (16, width), 1)
        place = (me * LOCAL + place).astype(F32)
        return jnp.exp(-decay_column * (place * (1.0 / SEQ)))

    def taps_row(r, carry):
        start = pl.multiple_of((core * 8 + r) * N + my_y * QUARTER, QUARTER)
        raw = fr[:, pl.ds(start, QUARTER)].astype(F32)
        made = (raw * envelope(start, QUARTER) * SCALE).astype(BF16)
        turned[pl.ds(pl.multiple_of(r * 16, 16), 16), 0:QUARTER] = made
        return carry

    lax.fori_loop(0, 8, taps_row, 0)
    swap = selection((128, 128), lambda i, j: j == (i % 8) * 16 + i // 8)
    arranged = dot(swap, turned[0:128, 0:QUARTER])
    send_t[...] = arranged.reshape(16, 8, QUARTER).astype(BF16)
    pl.semaphore_wait(barrier, 2 * CTX - 1 + 7)
    copy_t = small_exchange(0, send_t, taps_q.at[place])
    over(copy_t, "start")
    loads[0].wait()
    loads[1].wait()
    multiply(ig, va, mixed, send_m)
    copy_m = exchange(1, send_m, recv_m)
    over(copy_m, "start")
    loads[4].wait()
    loads[5].wait()
    multiply(ct, og, weighted, send_w)
    copy_w = exchange(2, send_w, recv_w)
    over(copy_w, "start")
    taps_q[pl.ds(place, 1), pl.ds(me, 1)] = send_t[pl.ds(me, 1)][None]
    keep(send_m, recv_m)
    keep(send_w, recv_w)

    loads[6].wait()
    loads[7].wait()
    loads[8].wait()
    cosine, sine = roots[0], roots[1]
    first[0:N, 0:HALF] = cosine[:, 0:HALF]
    first[0:N, HALF:N] = sine[:, 0:HALF]
    first[N:, 0:HALF] = -sine[:, 0:HALF]
    first[N:, HALF:N] = cosine[:, 0:HALF]
    first_back[0:HALF, 0:N] = cosine[0:HALF]
    first_back[0:HALF, N:] = -sine[0:HALF]
    first_back[HALF:, 0:N] = sine[0:HALF]
    first_back[HALF:, N:] = cosine[0:HALF]
    gather = selection(
        (256, 256), lambda i, j: j == ((i % 128) // 8) * 16 + (i // 128) * 8 + i % 8
    )
    scatter = selection(
        (256, 256), lambda i, j: i == ((j % 128) // 8) * 16 + (j // 128) * 8 + j % 8
    )
    first_taps[...] = dot(first[:, 0:HALF], scatter).astype(BF16)
    first_lag[...] = dot(gather, first_back[0:HALF, :]).astype(BF16)
    second[0:N, 0:N] = cosine
    second[0:N, N:] = -sine
    second[N:, 0:N] = sine
    second[N:, N:] = cosine
    second_back[0:N, 0:N] = cosine
    second_back[0:N, N:] = sine
    second_back[N:, 0:N] = -sine
    second_back[N:, N:] = cosine
    fine_r, fine_i = turns[0, 32:48, :], turns[1, 32:48, :]

    def turn_rows(a, carry):
        rows = pl.ds(pl.multiple_of(a * 16, 16), 16)
        tr, ti = times(turns[0, pl.ds(a, 1), :], turns[1, pl.ds(a, 1), :], fine_r, fine_i)
        wr[rows, :] = tr
        wi[rows, :] = ti
        return carry

    lax.fori_loop(0, N // 16, turn_rows, 0)

    over(copy_t, "wait_recv")

    share_t = among(0, lambda j: taps_q.at[place], taps_q)
    over(share_t, "start", 7)
    over(share_t, "wait_recv", 7)
    for p in range(8):
        y, half = p // 2, p % 2
        piece = taps_q[p].astype(F32).reshape(128, QUARTER).astype(BF16)
        taps[half * 128 : (half + 1) * 128, y * QUARTER : (y + 1) * QUARTER] = piece

    def forward(start, table, block):
        rows = pl.ds(start, CHUNK)
        pr = dot(table[rows, :], block)
        pi = dot(table[pl.ds(start + N, CHUNK), :], block)
        return dot(joined(*times(pr, pi, wr[rows, :], wi[rows, :])), second[...])

    def backward(start, spectrum, target):
        rows = pl.ds(start, CHUNK)
        br, bi = parts(dot(spectrum, second_back[...]))
        sr, si = conj_times(wr[rows, :], wi[rows, :], br, bi)
        target[rows, :] = (sr * (1.0 / FFT_LEN)).astype(BF16)
        target[pl.ds(start + N, CHUNK), :] = (si * (1.0 / FFT_LEN)).astype(BF16)

    def chunks(body):
        def one(i, carry):
            body(pl.multiple_of(i * CHUNK, CHUNK))
            return carry

        lax.fori_loop(0, N // CHUNK, one, 0)

    def filter_chunk(start):
        spec_h[pl.ds(start, CHUNK), :] = forward(start, first_taps, taps[...]).astype(BF16)

    chunks(filter_chunk)

    over(copy_m, "wait_recv")

    def mix_chunk(start):
        rows = pl.ds(start, CHUNK)
        spectrum = forward(start, first, recv_m[...].reshape(N, N))
        spec_m[rows, :] = spectrum
        hr, hi = parts(spec_h[rows, :].astype(F32))
        backward(start, joined(*times(*parts(spectrum), hr, hi)), turned)

    chunks(mix_chunk)
    for g in range(2):
        made = dot(first_back[g * HALF : (g + 1) * HALF, :], turned[...])
        send_c[g] = made.astype(BF16).reshape(16, 16, N)
    copy_c = exchange(3, send_c, recv_c)
    over(copy_c, "start")
    keep(send_c, recv_c)

    over(copy_w, "wait_recv")

    def weight_chunk(start):
        rows = pl.ds(start, CHUNK)
        spectrum = forward(start, first, recv_w[...].reshape(N, N))
        spec_w[rows, :] = spectrum
        mr, mi = parts(spec_m[rows, :])
        backward(start, joined(*conj_times(mr, mi, *parts(spectrum))), turned_lag)

    chunks(weight_chunk)
    lagged = dot(first_lag[...], turned_lag[...]).astype(BF16)
    for p in range(8):
        y, half = p // 2, p % 2
        lag_q[p] = lagged[half * 128 : (half + 1) * 128, y * QUARTER : (y + 1) * QUARTER]

    copy_s = among(1, lambda j: lag_q.at[plane_peer(j)[0]], lag_y)
    over(copy_s, "start", 7)
    lag_y[pl.ds(place, 1)] = lag_q[pl.ds(place, 1)]

    def correlate_chunk(start):
        rows = pl.ds(start, CHUNK)
        hr, hi = parts(spec_h[rows, :].astype(F32))
        backward(start, joined(*conj_times(hr, hi, *parts(spec_w[rows, :]))), turned)

    chunks(correlate_chunk)
    copy_u = [half_exchange(5 + g, g, send_u, recv_u) for g in range(2)]
    for g in range(2):
        made = dot(first_back[g * HALF : (g + 1) * HALF, :], turned[...])
        send_u[g] = made.astype(BF16).reshape(16, 16, N)
        if g == 0:
            over(copy_u[0], "start", 8)
    over(copy_s, "wait_recv", 7)
    reduced = sum(lag_y[p].astype(F32) for p in range(8))
    lag_z[...] = reduced.reshape(16, 8, QUARTER).astype(BF16)

    def copy_z(i):
        side, other = any_peer(i)
        return pltpu.make_async_remote_copy(
            src_ref=lag_z.at[other],
            dst_ref=lag_f.at[low, me],
            send_sem=lag_send.at[i],
            recv_sem=lag_recv.at[i],
            device_id=(side * 8 + place, other),
            device_id_type=MESH,
        )

    over(copy_z, "start", 2 * CTX - 1)
    over(copy_u[0], "start", begin=8)
    over(copy_u[1], "start")
    lag_f[pl.ds(low, 1), pl.ds(me, 1)] = lag_z[pl.ds(me, 1)][None]
    keep(send_u, recv_u)

    skip_column = column(skip[...], 32)

    def finish(g, recv, base, left, right, first_out, second_out):
        gain = skip_column[g * 16 : g * 16 + 16]
        summed[...] = dot(perm[...], recv[g].reshape(256, N))

        def block(r, carry):
            rows = pl.ds(pl.multiple_of(r * 16, 16), 16)
            lanes = pl.ds(pl.multiple_of(r * N, N), N)
            total = summed[rows, :] + gain * base[g, rows, :].astype(F32)
            place = slice(g * 16, g * 16 + 16)
            first_out[place, lanes] = (left[place, lanes].astype(F32) * total).astype(BF16)
            second_out[place, lanes] = (right[place, lanes].astype(F32) * total).astype(BF16)
            return carry

        lax.fori_loop(0, ROWS, block, 0)

    over(copy_c, "wait_recv")
    for g in range(2):
        finish(g, recv_c, mixed, og, ct, out, gog)
    over(copy_z, "wait_recv", 2 * CTX - 1)
    both = lag_f[0].astype(F32) + lag_f[1].astype(F32)
    lag_g[pl.ds(place, 1)] = both.reshape(128, QUARTER).astype(BF16)[None]
    copy_g = among(2, lambda j: lag_g.at[place], lag_g)
    over(copy_g, "start", 7)
    over(copy_u[0], "wait_recv")
    finish(0, recv_u, weighted, va, ig, gig, gva)
    over(copy_g, "wait_recv", 7)
    for p in range(8):
        y, half = p // 2, p % 2
        lag[half * 128 : (half + 1) * 128, y * QUARTER : (y + 1) * QUARTER] = lag_g[p]
    order = selection(
        (256, 256), lambda i, j: j == (i // 128) * 128 + (i % 16) * 8 + (i % 128) // 16
    )
    summed[...] = dot(order, lag[...])

    def filter_row(r, carry):
        start = pl.multiple_of(r * N, N)
        piece = summed[pl.ds(pl.multiple_of(r * 16, 16), 16), :]
        gf[:, pl.ds(start, N)] = piece * envelope(start, N) * SCALE
        return carry

    lax.fori_loop(0, ROWS, filter_row, 0)
    over(copy_u[1], "wait_recv")
    finish(1, recv_u, weighted, va, ig, gig, gva)
    for copy in (copy_t, copy_m, copy_w, copy_c, *copy_u):
        over(copy, "wait_send")
    for copy in (copy_s, copy_g):
        over(copy, "wait_send", 7)
    over(copy_z, "wait_send", 2 * CTX - 1)
    over(share_t, "wait_send", 7)


def store_kernel(*refs):
    copies = [
        pltpu.make_async_copy(source, target, refs[10].at[i])
        for i, (source, target) in enumerate(zip(refs[:5], refs[5:10]))
    ]
    for copy in copies:
        copy.start()
    for copy in copies:
        copy.wait()


def shards(input_gate, output_gate, values, cotangent, filter_raw, filter_decay, skip_gain):
    roots, turns = constant_tables()
    signal = pltpu.VMEM((32, LOCAL), BF16)
    blocks = pltpu.VMEM((2, CTX, ROWS, N), BF16)
    pieces = pltpu.VMEM((8, 128, QUARTER), BF16)
    kept = pltpu.VMEM((16, LOCAL), F32)
    inside = pl.BlockSpec(memory_space=pltpu.VMEM)
    anywhere = pl.BlockSpec(memory_space=pl.ANY)
    made = pl.pallas_call(
        kernel,
        out_shape=(signal, signal, signal, signal, kept),
        in_specs=[pl.BlockSpec(memory_space=pltpu.HBM)] * 9,
        out_specs=(inside,) * 5,
        scratch_shapes=[
            signal, signal, signal, signal,
            pltpu.VMEM((16, LOCAL), BF16),
            pltpu.VMEM((1, 16), F32),
            pltpu.VMEM((1, 32), F32),
            pltpu.VMEM((2, N, N), BF16),
            pltpu.VMEM((2, 48, N), F32),
            pltpu.VMEM((2 * N, N), BF16),
            pltpu.VMEM((N, 2 * N), BF16),
            pltpu.VMEM((HALF, 2 * N), BF16),
            pltpu.VMEM((2 * N, HALF), BF16),
            pltpu.VMEM((2 * N, 2 * N), BF16),
            pltpu.VMEM((2 * N, 2 * N), BF16),
            pltpu.VMEM((N, N), F32),
            pltpu.VMEM((N, N), F32),
            pltpu.VMEM((256, 256), BF16),
            pltpu.VMEM((2, 256, N), BF16),
            pltpu.VMEM((2, 256, N), BF16),
            blocks, blocks, blocks, blocks,
            pltpu.VMEM((CTX, 8, QUARTER), BF16),
            pltpu.VMEM((8, CTX, 8, QUARTER), BF16),
            pltpu.VMEM((256, N), BF16),
            pltpu.VMEM((N, 2 * N), BF16),
            pltpu.VMEM((N, 2 * N), F32),
            pltpu.VMEM((N, 2 * N), F32),
            pltpu.VMEM((2 * N, N), BF16),
            pltpu.VMEM((2 * N, N), BF16),
            blocks, blocks, blocks, blocks,
            pltpu.VMEM((256, N), F32),
            pieces,
            pieces,
            pltpu.VMEM((CTX, 8, QUARTER), BF16),
            pltpu.VMEM((2, CTX, 8, QUARTER), BF16),
            pieces,
            pltpu.VMEM((256, N), BF16),
            pltpu.SemaphoreType.DMA((9,)),
            pltpu.SemaphoreType.DMA((7, CTX - 1)),
            pltpu.SemaphoreType.DMA((7, CTX - 1)),
            pltpu.SemaphoreType.DMA((3, 7)),
            pltpu.SemaphoreType.DMA((3, 7)),
            pltpu.SemaphoreType.DMA((2 * CTX - 1,)),
            pltpu.SemaphoreType.DMA((2 * CTX - 1,)),
        ],
        compiler_params=pltpu.CompilerParams(
            collective_id=0, has_side_effects=True, vmem_limit_bytes=48 << 20
        ),
    )(
        *[
            pltpu.with_memory_space_constraint(x, pltpu.HBM)
            for x in (
                input_gate, values, cotangent, output_gate, filter_raw,
                filter_decay.reshape(1, 16), skip_gain.reshape(1, 32), jnp.asarray(roots), jnp.asarray(turns),
            )
        ]
    )
    big = jax.ShapeDtypeStruct((32, LOCAL), BF16)
    return pl.pallas_call(
        store_kernel,
        out_shape=(big, big, big, big, jax.ShapeDtypeStruct((16, LOCAL), F32)),
        in_specs=[inside] * 5,
        out_specs=(anywhere,) * 5,
        scratch_shapes=[pltpu.SemaphoreType.DMA((5,))],
        compiler_params=pltpu.CompilerParams(vmem_limit_bytes=8 << 20),
    )(*made)


def solution(mesh):
    return jax.shard_map(
        shards,
        mesh=mesh,
        in_specs=(
            P("dp", "ctx"),
            P("dp", "ctx"),
            P("dp", "ctx"),
            P("dp", "ctx"),
            P(None, "ctx"),
            P(),
            P("dp"),
        ),
        out_specs=(P("dp", "ctx"), P("dp", "ctx"), P("dp", "ctx"), P("dp", "ctx"), P(None, "ctx")),
        check_vma=False,
    )
```

time: 79.3 us -> 69.6 us (0.88)
  local copies, waits for them, and re-layouts: 6.41 us -> 0 us
  Pallas kernels: 71.7 us -> 68.8 us
    unnamed x13 -> x0, local copies, waits for them, and re-layouts: 6.41 us -> none
    pallas_call x1 -> x2, Pallas kernels: 71.7 us -> 68.8 us  [the longest x1 67.3 us: shards(): pl.pallas_call(kernel, out_shape=(signal, signal, signal, signal, kept),...]
where the time goes in v2:
time: 69.6 us; the launch traced here: 69.5 us
  Pallas kernels  68.8 us (99%)
    pallas_call x1, Pallas kernels, shards(): pl.pallas_call(kernel, out_shape=(signal, signal, signal, signal, kept),...  67.3 us
    pallas_call x1, Pallas kernels, shards(): pl.pallas_call(store_kernel, out_shape=(big, big, big, big, jax.ShapeDtyp...  1.53 us

profile of v2, /device:TPU:1, one launch (start us, length us, event | category | flops | bytes accessed | tf_op | source)
XLA Modules:
  0.0 69.5 jit_solution(15720304126834755728)
XLA Ops:
  0.6 67.3 %shard_map.128 = (bf16[32,8192]{1,0:T(8,128)(2,1)S(1)}, bf16[32,8192]{1,0:T(8,128)(2,1)S(1)}, bf16[32,8192]{1,0:T(8,128)(2,1)S(1)}, bf16[32,8192]{1,0:T(8,128)(2,1)S(1)}, f32[16,8192]{1,0:T(8,128)S(1)}) custom-call(bf16[32,8192]{1,0:T(8,128)(2,1)} %ig_hbm.1, bf16[32,8192]{1,0:T(8,128)(2,1)} %va_hbm.1, bf16[32,8192]{1,0:T(8,128)(2,1)} %ct_hbm.1, ...), custom_call_target="tpu_custom_call" | custom-call | tf_op jit(solution)/shard_map/pallas_call | solution.py:459
  67.9 1.5 %shard_map.129 = (bf16[32,8192]{1,0:T(8,128)(2,1)}, bf16[32,8192]{1,0:T(8,128)(2,1)}, bf16[32,8192]{1,0:T(8,128)(2,1)}, bf16[32,8192]{1,0:T(8,128)(2,1)}, f32[16,8192]{1,0:T(8,128)}) custom-call(bf16[32,8192]{1,0:T(8,128)(2,1)S(1)} %get-tuple-element.10.refs_0_, bf16[32,8192]{1,0:T(8,128)(2,1)S(1)} %get-tuple-element.11.refs_1_, ...), custom_call_target="tpu_custom_call" | custom-call | tf_op jit(solution)/shard_map/pallas_call | solution.py:520

commit v3 on v2

--- a/solution.py
+++ b/solution.py
@@ -88,23 +88,6 @@
         moved = ctx_peer(i % (CTX - 1)) - me
         return (low + (i + 1) // CTX) % 2, me + moved * (1 - i // (2 * CTX - 2))
 
-    barrier = pltpu.get_barrier_semaphore()
-
-    def greet(i, carry):
-        side, other = any_peer(i)
-        device = (side * 8 + dp % 8, other)
-        pl.semaphore_signal(barrier, inc=1, device_id=device, device_id_type=MESH)
-        return carry
-
-    def greet_plane(j, carry):
-        pl.semaphore_signal(
-            barrier, inc=1, device_id={"dp": plane_peer(j)[1]}, device_id_type=MESH
-        )
-        return carry
-
-    lax.fori_loop(0, 2 * CTX - 1, greet, 0)
-    lax.fori_loop(0, 7, greet_plane, 0)
-
     loads = [
         pltpu.make_async_copy(source, target, in_sem.at[i])
         for i, (source, target) in enumerate(
@@ -117,6 +100,23 @@
     for load in loads:
         load.start()
 
+    barrier = pltpu.get_barrier_semaphore()
+
+    def greet(i, carry):
+        side, other = any_peer(i)
+        device = (side * 8 + dp % 8, other)
+        pl.semaphore_signal(barrier, inc=1, device_id=device, device_id_type=MESH)
+        return carry
+
+    def greet_plane(j, carry):
+        pl.semaphore_signal(
+            barrier, inc=1, device_id={"dp": plane_peer(j)[1]}, device_id_type=MESH
+        )
+        return carry
+
+    lax.fori_loop(0, 2 * CTX - 1, greet, 0)
+    lax.fori_loop(0, 7, greet_plane, 0)
+
     def selection(shape, where):
         row = lax.broadcasted_iota(jnp.int32, shape, 0)
         col = lax.broadcasted_iota(jnp.int32, shape, 1)
@@ -139,7 +139,7 @@
                 target[g, pl.ds(pl.multiple_of(r * 16, 16), 16), :] = (a * b).astype(BF16)
                 return carry
 
-            lax.fori_loop(0, ROWS, block, 0)
+            lax.fori_loop(0, ROWS, block, 0, unroll=4)
             send[g] = dot(perm[...], target[g]).astype(BF16).reshape(16, 16, N)
 
     def exchange(k, send, recv):
@@ -399,7 +399,7 @@
             second_out[place, lanes] = (right[place, lanes].astype(F32) * total).astype(BF16)
             return carry
 
-        lax.fori_loop(0, ROWS, block, 0)
+        lax.fori_loop(0, ROWS, block, 0, unroll=4)
 
     over(copy_c, "wait_recv")
     for g in range(2):
@@ -427,14 +427,13 @@
         return carry
 
     lax.fori_loop(0, ROWS, filter_row, 0)
+    for copy in (copy_t, copy_m, copy_w, copy_c, *copy_u):
+        over(copy, "wait_send")
+    for copy in (copy_s, copy_g, share_t):
+        over(copy, "wait_send", 7)
+    over(copy_z, "wait_send", 2 * CTX - 1)
     over(copy_u[1], "wait_recv")
     finish(1, recv_u, weighted, va, ig, gig, gva)
-    for copy in (copy_t, copy_m, copy_w, copy_c, *copy_u):
-        over(copy, "wait_send")
-    for copy in (copy_s, copy_g):
-        over(copy, "wait_send", 7)
-    over(copy_z, "wait_send", 2 * CTX - 1)
-    over(share_t, "wait_send", 7)
 
 
 def store_kernel(*refs):

time: 69.6 us -> 68.5 us (0.984)
  Pallas kernels: 68.8 us -> 67.8 us
    pallas_call x1, Pallas kernels: 67.3 us -> 66.3 us  [shards(): pl.pallas_call(kernel, out_shape=(signal, signal, signal, signal, kept),...]
where the time goes in v3:
time: 68.5 us; the launch traced here: 68.4 us
  Pallas kernels  67.8 us (99%)
    pallas_call x1, Pallas kernels, shards(): pl.pallas_call(kernel, out_shape=(signal, signal, signal, signal, kept),...  66.3 us
    pallas_call x1, Pallas kernels, shards(): pl.pallas_call(store_kernel, out_shape=(big, big, big, big, jax.ShapeDtyp...  1.53 us

profile of v3, /device:TPU:1, one launch (start us, length us, event | category | flops | bytes accessed | tf_op | source)
XLA Modules:
  0.0 68.4 jit_solution(11697499670462157983)
XLA Ops:
  0.6 66.3 %shard_map.128 = (bf16[32,8192]{1,0:T(8,128)(2,1)S(1)}, bf16[32,8192]{1,0:T(8,128)(2,1)S(1)}, bf16[32,8192]{1,0:T(8,128)(2,1)S(1)}, bf16[32,8192]{1,0:T(8,128)(2,1)S(1)}, f32[16,8192]{1,0:T(8,128)S(1)}) custom-call(bf16[32,8192]{1,0:T(8,128)(2,1)} %ig_hbm.1, bf16[32,8192]{1,0:T(8,128)(2,1)} %va_hbm.1, bf16[32,8192]{1,0:T(8,128)(2,1)} %ct_hbm.1, ...), custom_call_target="tpu_custom_call" | custom-call | tf_op jit(solution)/shard_map/pallas_call | solution.py:458
  66.9 1.5 %shard_map.129 = (bf16[32,8192]{1,0:T(8,128)(2,1)}, bf16[32,8192]{1,0:T(8,128)(2,1)}, bf16[32,8192]{1,0:T(8,128)(2,1)}, bf16[32,8192]{1,0:T(8,128)(2,1)}, f32[16,8192]{1,0:T(8,128)}) custom-call(bf16[32,8192]{1,0:T(8,128)(2,1)S(1)} %get-tuple-element.10.refs_0_, bf16[32,8192]{1,0:T(8,128)(2,1)S(1)} %get-tuple-element.11.refs_1_, ...), custom_call_target="tpu_custom_call" | custom-call | tf_op jit(solution)/shard_map/pallas_call | solution.py:519

commit v4 on v3

--- a/solution.py
+++ b/solution.py
@@ -204,6 +204,7 @@
     def keep(send, recv):
         recv[:, pl.ds(me, 1)] = send[:, pl.ds(me, 1)]
 
+    swap = selection((128, 128), lambda i, j: j == (i % 8) * 16 + i // 8)
     loads[2].wait()
     loads[3].wait()
     decay_column = column(decay[...], 16)
@@ -221,7 +222,6 @@
         return carry
 
     lax.fori_loop(0, 8, taps_row, 0)
-    swap = selection((128, 128), lambda i, j: j == (i % 8) * 16 + i // 8)
     arranged = dot(swap, turned[0:128, 0:QUARTER])
     send_t[...] = arranged.reshape(16, 8, QUARTER).astype(BF16)
     pl.semaphore_wait(barrier, 2 * CTX - 1 + 7)
@@ -404,6 +404,9 @@
     over(copy_c, "wait_recv")
     for g in range(2):
         finish(g, recv_c, mixed, og, ct, out, gog)
+    order = selection(
+        (256, 256), lambda i, j: j == (i // 128) * 128 + (i % 16) * 8 + (i % 128) // 16
+    )
     over(copy_z, "wait_recv", 2 * CTX - 1)
     both = lag_f[0].astype(F32) + lag_f[1].astype(F32)
     lag_g[pl.ds(place, 1)] = both.reshape(128, QUARTER).astype(BF16)[None]
@@ -415,9 +418,6 @@
     for p in range(8):
         y, half = p // 2, p % 2
         lag[half * 128 : (half + 1) * 128, y * QUARTER : (y + 1) * QUARTER] = lag_g[p]
-    order = selection(
-        (256, 256), lambda i, j: j == (i // 128) * 128 + (i % 16) * 8 + (i % 128) // 16
-    )
     summed[...] = dot(order, lag[...])
 
     def filter_row(r, carry):

time: 68.5 us -> 68.5 us (level)
  no operation moved by 1% of the time
where the time goes in v4:
time: 68.5 us; the launch traced here: 68.4 us
  Pallas kernels  67.8 us (99%)
    pallas_call x1, Pallas kernels, shards(): pl.pallas_call(kernel, out_shape=(signal, signal, signal, signal, kept),...  66.2 us
    pallas_call x1, Pallas kernels, shards(): pl.pallas_call(store_kernel, out_shape=(big, big, big, big, jax.ShapeDtyp...  1.53 us

profile of v4, /device:TPU:1, one launch (start us, length us, event | category | flops | bytes accessed | tf_op | source)
XLA Modules:
  0.0 68.4 jit_solution(17057370523842358407)
XLA Ops:
  0.6 66.2 %shard_map.128 = (bf16[32,8192]{1,0:T(8,128)(2,1)S(1)}, bf16[32,8192]{1,0:T(8,128)(2,1)S(1)}, bf16[32,8192]{1,0:T(8,128)(2,1)S(1)}, bf16[32,8192]{1,0:T(8,128)(2,1)S(1)}, f32[16,8192]{1,0:T(8,128)S(1)}) custom-call(bf16[32,8192]{1,0:T(8,128)(2,1)} %ig_hbm.1, bf16[32,8192]{1,0:T(8,128)(2,1)} %va_hbm.1, bf16[32,8192]{1,0:T(8,128)(2,1)} %ct_hbm.1, ...), custom_call_target="tpu_custom_call" | custom-call | tf_op jit(solution)/shard_map/pallas_call | solution.py:458
  66.9 1.5 %shard_map.129 = (bf16[32,8192]{1,0:T(8,128)(2,1)}, bf16[32,8192]{1,0:T(8,128)(2,1)}, bf16[32,8192]{1,0:T(8,128)(2,1)}, bf16[32,8192]{1,0:T(8,128)(2,1)}, f32[16,8192]{1,0:T(8,128)}) custom-call(bf16[32,8192]{1,0:T(8,128)(2,1)S(1)} %get-tuple-element.10.refs_0_, bf16[32,8192]{1,0:T(8,128)(2,1)S(1)} %get-tuple-element.11.refs_1_, ...), custom_call_target="tpu_custom_call" | custom-call | tf_op jit(solution)/shard_map/pallas_call | solution.py:519
